TPU v7x, 32 devices: a whole 2x2x4 slice. The times are simulated.
32 devices in a mesh: groups: 2 (over y), brick: 4 (over z), chan: 2 (over x), sub: 2 (over core).
Axes of the slice: x: 2, y: 2, z: 4, core: 2. Of those that a mesh axis runs over, the one named last changes fastest.
Arguments:
- features: bfloat16 [16384, 256], P(('groups', 'brick', 'chan', 'sub')), parts along dimension 0, may hold values from -6 to 6
- scan_order: int32 [32, 512], P(('groups', 'brick', 'chan', 'sub')), parts along dimension 0, may hold values from 0 to 511, each once within a row
- kernel_map: int32 [256, 27], P(('groups', 'brick', 'sub')), parts along dimension 0, may hold values from 0 to 20, as said below
- halo_send: int32 [32, 2], P(('groups', 'brick', 'sub')), parts along dimension 0, may hold values from 0 to 15, as said below
- down_route: int32 [256, 1], P(('groups', 'brick', 'sub')), parts along dimension 0, may hold values from 0 to 7; in each aligned block of 16 rows (0 to 15, 16 to 31, ...) at most 4 rows name the same one
- conv1_weight: bfloat16 [27, 256, 256], P(None, 'chan'), may hold values from -0.078125 to 0.078125
- conv2_weight: bfloat16 [27, 256, 256], P(None, 'chan'), may hold values from -0.078125 to 0.078125
- down_weight: bfloat16 [8, 256, 256], P(None, 'chan'), may hold values from -0.125 to 0.125
- gain_first: float32 [256], P('chan'), may hold values from 0.1 to 1.9
- bias_first: float32 [256], P('chan'), may hold values from -3 to 3
- gain_second: float32 [256], P('chan'), may hold values from 0.1 to 1.9
- bias_second: float32 [256], P('chan'), may hold values from -3 to 3
- gain_down: float32 [256], P('chan'), may hold values from 0.1 to 1.9
- bias_down: float32 [256], P('chan'), may hold values from -3 to 3
Outputs:
- coarse_out: bfloat16 [16, 256, 256], P(('groups', 'brick', 'sub'), 'chan'), parts along dimension 0
There are 2 independent parts, one for each index of `groups`. A program takes and returns all parts, laid end to end along the dimension named above; an argument that names none is the same for every part. Nothing has to cross between parts.
Inputs may be any that keep to these rules, and one draw needn't show every extreme that they name: `scan_order`: each row is an order of the 512 local rows of one device, each once. `kernel_map`: entries index an owner's extended list: own blocks below 16, then 2 blocks from the previous owner, 2 from the next, and 20 for an absent neighbour block. Offset 13 of block n always names n itself. `halo_send`: row 2 o lists the blocks owner o sends to owner o + 1, row 2 o + 1 those it sends to owner o - 1; each row names 2 distinct blocks. `down_route`: within the 16 rows of one owner no destination is named by more than 4 rows.
All inputs are finite; a program needn't handle non-finite values.
Results may differ from a plain program's by a relative error of at most 0.014.
Values may be sent and summed in bfloat16 or wider, within the bound.
A program may use at most 64 MiB of HBM per device.

v0:
```python
import functools

import jax
import jax.numpy as jnp
from jax import lax
from jax.experimental import pallas as pl
from jax.experimental.pallas import tpu as pltpu
from jax.sharding import PartitionSpec as P

BLK = 64
LANES = 128
MESH = pl.DeviceIdType.MESH


def products(lhs, weight, prod, place):
    width = prod.shape[3]
    shape = (lhs.shape[0] // BLK, BLK, width)

    def step(pair, carry):
        both = weight[pl.ds(pl.multiple_of(pair * 2 * width, 2 * width), 2 * width), :]
        result = lax.dot_general(
            lhs, both, (((1,), (1,)), ((), ())), preferred_element_type=jnp.float32
        )
        prod[2 * pair, place] = result[:, :width].reshape(shape)
        prod[2 * pair + 1, place] = result[:, width:].reshape(shape)
        return carry

    lax.fori_loop(0, prod.shape[0] // 2, step, 0, unroll=True)


def gathered_sum(prod, kernel_map, n):
    total = None
    for k in range(kernel_map.shape[1]):
        term = prod[k, kernel_map[n, k]]
        total = term if total is None else total + term
    return total


def flip(x, bits):
    result = x
    weight = 1
    while weight <= bits:
        if bits & weight:
            result = result + weight - 2 * weight * lax.rem(lax.div(x, weight), 2)
        weight *= 2
    return result


def fused_kernel(
    axes,
    features_hbm,
    scan_order_hbm,
    kernel_map_hbm,
    halo_send_hbm,
    down_route_hbm,
    conv1_hbm,
    conv2_hbm,
    down_hbm,
    gain_first_hbm,
    bias_first_hbm,
    gain_second_hbm,
    bias_second_hbm,
    gain_down_hbm,
    bias_down_hbm,
    out,
    features,
    scan_order,
    kernel_map,
    halo_send,
    down_route,
    gain_first,
    bias_first,
    gain_second,
    bias_second,
    gain_down,
    bias_down,
    stage_sem,
    conv1_w,
    conv2_w,
    down_w,
    ordered,
    ext,
    halo_out,
    halo_in,
    hid_own,
    hid_in,
    hid_halo_out,
    hid_halo_in,
    prod,
    kids_ref,
    part,
    part_out,
    part_in,
    tile_out,
    tile_in,
    w_sem,
    a2a_s,
    a2a_r,
    fwd_s,
    fwd_r,
    halo_s,
    halo_r,
    hid_s,
    hid_r,
    hh_s,
    hh_r,
    part_s,
    part_r,
    tile_s,
    tile_r,
):
    staged = [
        pltpu.make_async_copy(source, place, stage_sem.at[i])
        for i, (source, place) in enumerate(
            [
                (features_hbm, features),
                (scan_order_hbm, scan_order),
                (kernel_map_hbm, kernel_map),
                (halo_send_hbm, halo_send),
                (down_route_hbm, down_route),
                (gain_first_hbm, gain_first),
                (bias_first_hbm, bias_first),
                (gain_second_hbm, gain_second),
                (bias_second_hbm, bias_second),
                (gain_down_hbm, gain_down),
                (bias_down_hbm, bias_down),
            ]
        )
    ]
    for load in staged:
        load.start()
    n_brick, n_chan, n_sub = axes
    owners = n_brick * n_sub
    blocks = kernel_map.shape[0]
    channels = features.shape[1]
    width = out.shape[1]
    hcap = halo_send.shape[1]
    group_count = hid_s.shape[1]
    group = blocks // group_count
    me_group = lax.axis_index("groups")
    chan = lax.axis_index("chan")
    me = lax.axis_index("brick") * n_sub + lax.axis_index("sub")
    own_cols = pl.ds(pl.multiple_of(chan * width, LANES), width)

    def device(owner, c):
        return (me_group, lax.div(owner, n_sub), c, lax.rem(owner, n_sub))

    def owner_at(shift):
        return lax.rem(me + shift + owners, owners)

    def chan_at(shift):
        return lax.rem(chan + shift + n_chan, n_chan)

    def remote(src, dst, send, recv, target):
        return pltpu.make_async_remote_copy(
            src_ref=src,
            dst_ref=dst,
            send_sem=send,
            recv_sem=recv,
            device_id=target,
            device_id_type=MESH,
        )

    taps = kernel_map.shape[1]
    loads = [
        pltpu.make_async_copy(conv1_hbm, conv1_w.at[pl.ds(0, taps * width)], w_sem.at[0]),
        pltpu.make_async_copy(down_hbm, down_w, w_sem.at[1]),
    ]

    def cols_from(j):
        return pl.ds(pl.multiple_of(chan_at(-j) * width, LANES), width)

    for j in range(n_chan):
        target = conv2_w.at[pl.ds(0, taps * width), pl.ds(j * width, width)]
        loads.append(
            pltpu.make_async_copy(conv2_hbm.at[:, cols_from(j)], target, w_sem.at[2 + j])
        )
    barrier = pltpu.get_barrier_semaphore()
    partners = [device(flip(me, i), chan) for i in range(1, owners)]
    partners += [device(me, chan_at(j)) for j in range(1, n_chan)]
    partners += [device(owner_at(d), chan_at(j)) for j in range(1, n_chan) for d in (1, -1)]
    for partner in partners:
        pl.semaphore_signal(barrier, inc=1, device_id=partner, device_id_type=MESH)
    for load in loads:
        load.start()

    spare = conv1_w.shape[0] - taps * width
    if spare:
        conv1_w[pl.ds(taps * width, spare), :] = jnp.zeros((spare, channels), jnp.bfloat16)
        conv2_w[pl.ds(taps * width, spare), :] = jnp.zeros((spare, channels), jnp.bfloat16)
    for k in range(taps):
        prod[k, blocks + 2 * hcap] = jnp.zeros((BLK, width), jnp.float32)

    for load in staged[:2]:
        load.wait()
    count = features.shape[0]
    source_row = lax.broadcasted_iota(jnp.int32, (count, count), 0)
    chosen = jnp.where(source_row == scan_order[...], 1.0, 0.0).astype(jnp.bfloat16)
    rows = lax.dot_general(
        chosen, features[...], (((0,), (0,)), ((), ())), preferred_element_type=jnp.float32
    ).astype(jnp.bfloat16)
    ordered[...] = rows.reshape(owners, BLK, channels)

    pl.semaphore_wait(barrier, len(partners))

    pending = []
    a2a = []
    for i in range(1, owners):
        target = flip(me, i)
        a2a.append(
            remote(
                ordered.at[target],
                ext.at[me * n_chan + chan],
                a2a_s.at[i - 1],
                a2a_r.at[i - 1],
                device(target, chan),
            )
        )
    for copy in a2a:
        copy.start()
    pending += a2a

    def forward(i, src):
        block = flip(me, i) * n_chan + chan
        for j in range(1, n_chan):
            copy = remote(
                src,
                ext.at[block],
                fwd_s.at[j - 1, i],
                fwd_r.at[j - 1, i],
                device(me, chan_at(j)),
            )
            copy.start()
            forwards[i].append(copy)

    forwards = [[] for _ in range(owners)]
    brick_blocks = n_sub * n_chan

    def pass_on(m):
        for i in range(m * n_sub, (m + 1) * n_sub):
            if i == 0:
                forward(0, ordered.at[me])
                ext[me * n_chan + chan] = ordered[me]
            else:
                a2a[i - 1].wait_recv()
                forward(i, ext.at[flip(me, i) * n_chan + chan])

    def collect(m):
        for i in range(m * n_sub, (m + 1) * n_sub):
            for copy in forwards[i]:
                copy.wait_recv()

    def multiply(m):
        place = pl.ds(flip(lax.axis_index("brick"), m) * brick_blocks, brick_blocks)
        products(ext[place].reshape(brick_blocks * BLK, channels), conv1_w, prod, place)

    pass_on(0)
    for load in staged[2:]:
        load.wait()
    loads[0].wait()
    for m in range(1, n_brick):
        pass_on(m)
        collect(m - 1)
        multiply(m - 1)
    collect(n_brick - 1)
    pending += [copy for copies in forwards for copy in copies]

    has_next, has_last = me < owners - 1, me > 0

    def halo_copies(direction):
        return remote(
            halo_out.at[direction],
            halo_in.at[direction],
            halo_s.at[direction],
            halo_r.at[direction],
            device(owner_at(1 if direction == 0 else -1), chan),
        )

    for direction, sends in ((0, has_next), (1, has_last)):
        for j in range(hcap):
            halo_out[direction, j] = ext[halo_send[direction, j]]
        pl.when(sends)(lambda direction=direction: halo_copies(direction).start())
    multiply(n_brick - 1)
    for direction, receives in ((0, has_last), (1, has_next)):

        @pl.when(receives)
        def _():
            halo_copies(direction).wait_recv()

        @pl.when(jnp.logical_not(receives))
        def _():
            halo_in[direction] = jnp.zeros((hcap, BLK, channels), jnp.bfloat16)

    rim = pl.ds(blocks, 2 * hcap)
    products(halo_in[...].reshape(2 * hcap * BLK, channels), conv1_w, prod, rim)

    def first_hidden(n):
        scaled = gathered_sum(prod, kernel_map, n) * gain_first[...] + bias_first[...]
        return jnp.maximum(scaled, 0.0).astype(jnp.bfloat16)

    def hid_halo_copies(direction):
        return [
            remote(
                hid_halo_out.at[direction],
                hid_halo_in.at[direction, j],
                hh_s.at[direction, j],
                hh_r.at[direction, j],
                device(owner_at(1 if direction == 0 else -1), chan_at(j)),
            )
            for j in range(n_chan)
        ]

    for direction, sends in ((0, has_next), (1, has_last)):
        for j in range(hcap):
            hid_halo_out[direction, j] = first_hidden(halo_send[direction, j])

        @pl.when(sends)
        def _():
            for copy in hid_halo_copies(direction):
                copy.start()

    hid_copies = []
    for g in range(group_count):

        def first_block(n, carry):
            hid_own[n] = first_hidden(n)
            return carry

        lax.fori_loop(g * group, (g + 1) * group, first_block, 0)
        place = pl.ds(g * group, group)
        for j in range(1, n_chan):
            copy = remote(
                hid_own.at[place],
                hid_in.at[j - 1, place],
                hid_s.at[j - 1, g],
                hid_r.at[j - 1, g],
                device(me, chan_at(j)),
            )
            copy.start()
            hid_copies.append(copy)
    pending += hid_copies

    for load in loads[2:]:
        load.wait()
    def second_products(g):
        place = pl.ds(g * group, group)
        halves = [hid_own[place]]
        for j in range(1, n_chan):
            hid_copies[g * (n_chan - 1) + j - 1].wait_recv()
            halves.append(hid_in[j - 1, place])
        lhs = jnp.concatenate([half.reshape(group * BLK, width) for half in halves], axis=1)
        products(lhs, conv2_w, prod, place)

    for g in range(group_count - 1):
        second_products(g)
    for direction, receives in ((0, has_last), (1, has_next)):

        @pl.when(receives)
        def _():
            for copy in hid_halo_copies(direction):
                copy.wait_recv()

        @pl.when(jnp.logical_not(receives))
        def _():
            hid_halo_in[direction] = jnp.zeros(hid_halo_in.shape[1:], jnp.bfloat16)

    halves = [hid_halo_in[:, j].reshape(2 * hcap * BLK, width) for j in range(n_chan)]
    products(jnp.concatenate(halves, axis=1), conv2_w, prod, rim)
    second_products(group_count - 1)
    loads[1].wait()
    kids = down_w.shape[0]
    cells = BLK // kids

    def second_block(n, carry):
        second = gathered_sum(prod, kernel_map, n)
        residual = ext[n, :, own_cols].astype(jnp.float32)
        refined = jnp.maximum(second * gain_second[...] + bias_second[...] + residual, 0.0)
        refined = refined.reshape(kids, cells, width)
        for o in range(kids):
            kids_ref[o, n] = refined[o]
        return carry

    lax.fori_loop(0, blocks, second_block, 0)
    partial = None
    for o in range(kids):
        child = kids_ref[o].reshape(blocks * cells, width).astype(jnp.bfloat16)
        product = jnp.dot(child, down_w[o], preferred_element_type=jnp.float32)
        partial = product if partial is None else partial + product
    part[...] = partial
    part_copies = []
    for j in range(1, n_chan):
        cols = pl.ds(pl.multiple_of(chan_at(j) * width, LANES), width)
        part_out[j - 1] = part[:, cols].astype(jnp.bfloat16)
        copy = remote(
            part_out.at[j - 1],
            part_in.at[j - 1],
            part_s.at[j - 1],
            part_r.at[j - 1],
            device(me, chan_at(j)),
        )
        copy.start()
        part_copies.append(copy)
    pending += part_copies

    slots = tile_out.shape[1]
    capacity = slots // cells
    column = lax.broadcasted_iota(jnp.int32, (1, blocks * cells), 1)
    target_row = lax.rem(column, cells)
    names = [down_route[0, n] for n in range(blocks)]
    for n in range(blocks):
        earlier = jnp.int32(0)
        for before in range(n):
            earlier = earlier + jnp.where(names[before] == names[n], 1, 0)
        position = (names[n] * capacity + earlier) * cells
        target_row = target_row + jnp.where(lax.div(column, cells) == n, position, 0)
    slot_row = lax.broadcasted_iota(jnp.int32, (owners * slots, blocks * cells), 0)
    selector = jnp.where(slot_row == target_row, 1.0, 0.0).astype(jnp.bfloat16)

    coarse = part[:, own_cols]
    for j in range(1, n_chan):
        part_copies[j - 1].wait_recv()
        coarse = coarse + part_in[j - 1].astype(jnp.float32)
    tiles = jnp.maximum(coarse * gain_down[...] + bias_down[...], 0.0).astype(jnp.bfloat16)
    outgoing = jnp.dot(selector, tiles, preferred_element_type=jnp.float32)
    tile_out[...] = outgoing.astype(jnp.bfloat16).reshape(owners, slots, width)
    tile_copies = []
    for i in range(1, owners):
        target = flip(me, i)
        copy = remote(
            tile_out.at[target],
            tile_in.at[me],
            tile_s.at[i - 1],
            tile_r.at[i - 1],
            device(target, chan),
        )
        copy.start()
        tile_copies.append(copy)
    pending += tile_copies
    tile_in[me] = tile_out[me]
    for copy in pending[: -len(tile_copies)]:
        copy.wait_send()
    for direction, sends in ((0, has_next), (1, has_last)):

        @pl.when(sends)
        def _():
            halo_copies(direction).wait_send()
            for copy in hid_halo_copies(direction):
                copy.wait_send()

    for copy in tile_copies:
        copy.wait_recv()
    arrived = tile_in[...].reshape(owners * slots, width).astype(jnp.float32)
    out[0] = arrived.T.astype(jnp.bfloat16)
    for copy in tile_copies:
        copy.wait_send()


def fused(axes, features, scan_order, kernel_map, halo_send, down_route, w1, w2, wd, *scales):
    n_brick, n_chan, n_sub = axes
    owners = n_brick * n_sub
    blocks = kernel_map.shape[0]
    channels = features.shape[1]
    width = w1.shape[1]
    hcap = halo_send.shape[1]
    taps = kernel_map.shape[1]
    even_taps = taps + taps % 2
    cells = BLK // wd.shape[0]
    slots = max(2, 2 * blocks // owners) * cells
    groups = 4
    bf16, f32 = jnp.bfloat16, jnp.float32
    vmem = pl.BlockSpec(memory_space=pltpu.VMEM)
    hbm = pl.BlockSpec(memory_space=pl.ANY)

    def pair(*shape):
        return [pltpu.SemaphoreType.DMA(shape), pltpu.SemaphoreType.DMA(shape)]

    return pl.pallas_call(
        functools.partial(fused_kernel, axes),
        out_shape=jax.ShapeDtypeStruct((1, width, owners * slots), bf16),
        in_specs=[hbm] * 14,
        out_specs=vmem,
        scratch_shapes=[
            pltpu.VMEM(features.shape, bf16),
            pltpu.VMEM(scan_order.shape, jnp.int32),
            pltpu.SMEM(kernel_map.shape, jnp.int32),
            pltpu.SMEM(halo_send.shape, jnp.int32),
            pltpu.SMEM((1, blocks), jnp.int32),
            *[pltpu.VMEM((1, width), f32)] * 6,
            pltpu.SemaphoreType.DMA((11,)),
            pltpu.VMEM((even_taps * width, channels), bf16),
            pltpu.VMEM((even_taps * width, channels), bf16),
            pltpu.VMEM(wd.shape, bf16),
            pltpu.VMEM((owners, BLK, channels), bf16),
            pltpu.VMEM((blocks, BLK, channels), bf16),
            pltpu.VMEM((2, hcap, BLK, channels), bf16),
            pltpu.VMEM((2, hcap, BLK, channels), bf16),
            pltpu.VMEM((blocks, BLK, width), bf16),
            pltpu.VMEM((n_chan - 1, blocks, BLK, width), bf16),
            pltpu.VMEM((2, hcap, BLK, width), bf16),
            pltpu.VMEM((2, n_chan, hcap, BLK, width), bf16),
            pltpu.VMEM((even_taps, blocks + 2 * hcap + 1, BLK, width), f32),
            pltpu.VMEM((wd.shape[0], blocks, cells, width), f32),
            pltpu.VMEM((blocks * cells, channels), f32),
            pltpu.VMEM((n_chan - 1, blocks * cells, width), bf16),
            pltpu.VMEM((n_chan - 1, blocks * cells, width), bf16),
            pltpu.VMEM((owners, slots, width), bf16),
            pltpu.VMEM((owners, slots, width), bf16),
            pltpu.SemaphoreType.DMA((2 + n_chan,)),
            *pair(owners - 1),
            *pair(n_chan - 1, owners),
            *pair(2),
            *pair(n_chan - 1, groups),
            *pair(2, n_chan),
            *pair(n_chan - 1),
            *pair(owners - 1),
        ],
        compiler_params=pltpu.CompilerParams(
            collective_id=0, has_side_effects=True, vmem_limit_bytes=67043328
        ),
        name="encoder_level",
    )(
        features,
        scan_order,
        kernel_map,
        halo_send,
        down_route.reshape(1, blocks),
        w1.reshape(taps * width, channels),
        w2.reshape(taps * width, channels),
        wd,
        *[scale.reshape(1, width) for scale in scales],
    )


def fits(axes, features, kernel_map, width):
    n_brick, n_chan, n_sub = axes
    owners = n_brick * n_sub
    whole = width % LANES == 0 and n_chan > 1 and kernel_map.shape[0] % 4 == 0
    whole = whole and owners & (owners - 1) == 0 and n_sub & (n_sub - 1) == 0
    return whole and features.shape[0] == owners * BLK and kernel_map.shape[0] == owners * n_chan


def from_behind(block, axis, distance):
    devices = range(lax.axis_size(axis))
    route = [(i - distance, i) for i in devices if i - distance in devices]
    return lax.ppermute(block, axis, route)


def neighbours(blocks, step_by):
    return from_behind(blocks, ("brick", "sub"), step_by)


def convolve(extended, weight, kernel_map, pattern):
    block_count = kernel_map.shape[0]
    width_out = weight.shape[1]
    groups = weight.shape[0] // 3
    weight_groups = weight.reshape(groups, 3, width_out, weight.shape[2])
    index_groups = kernel_map.T.reshape(groups, 3, block_count)
    offsets = jnp.arange(3, dtype=jnp.int32)[:, None]

    def one_group(running, inputs):
        group_weight, indices = inputs
        product = jnp.einsum(pattern, group_weight, extended, preferred_element_type=jnp.float32)
        return (running + jnp.sum(product[offsets, :, indices], axis=0), None)

    initial = jnp.zeros((block_count, width_out, BLK), jnp.float32)
    running, _ = lax.scan(one_group, initial, (weight_groups, index_groups))
    return running.transpose(1, 0, 2).reshape(width_out, block_count * BLK)


def body(
    features,
    scan_order,
    kernel_map,
    halo_send,
    down_route,
    conv1_weight,
    conv2_weight,
    down_weight,
    gain_first,
    bias_first,
    gain_second,
    bias_second,
    gain_down,
    bias_down,
):
    axes = tuple(lax.axis_size(name) for name in ("brick", "chan", "sub"))
    if fits(axes, features, kernel_map, conv1_weight.shape[1]):
        return fused(
            axes,
            features,
            scan_order,
            kernel_map,
            halo_send,
            down_route,
            conv1_weight,
            conv2_weight,
            down_weight,
            gain_first,
            bias_first,
            gain_second,
            bias_second,
            gain_down,
            bias_down,
        )
    owners = lax.axis_size(("brick", "sub"))
    per_owner = features.shape[0] // owners
    channels = features.shape[1]
    width_out = conv1_weight.shape[1]
    block_count = kernel_map.shape[0]
    channel_start = lax.axis_index("chan") * width_out
    ordered = features[scan_order[0]].reshape(owners, per_owner, channels)
    regrouped = lax.all_to_all(ordered, ("brick", "sub"), split_axis=0, concat_axis=0, tiled=True)
    owner_rows = lax.all_gather(regrouped, "chan", axis=1, tiled=True)
    row_blocks = owner_rows.reshape(block_count, BLK, channels)
    from_lower = neighbours(row_blocks[halo_send[0]], 1)
    from_upper = neighbours(row_blocks[halo_send[1]], -1)
    empty_rows = jnp.zeros((1, BLK, channels), jnp.bfloat16)
    extended = jnp.concatenate([row_blocks, from_lower, from_upper, empty_rows], axis=0)
    conv_first = convolve(extended, conv1_weight, kernel_map, "kdc,brc->kdbr")
    hidden = jax.nn.relu(conv_first * gain_first[:, None] + bias_first[:, None]).astype(
        jnp.bfloat16
    )
    hidden_blocks = hidden.reshape(width_out, block_count, BLK)
    empty_cols = jnp.zeros((channels, 1, BLK), jnp.bfloat16)
    all_channels = lax.all_gather(hidden_blocks, "chan", axis=0, tiled=True)
    lower_cols = neighbours(all_channels[:, halo_send[0]], 1)
    upper_cols = neighbours(all_channels[:, halo_send[1]], -1)
    widened_hidden = jnp.concatenate([all_channels, lower_cols, upper_cols, empty_cols], axis=1)
    second = convolve(widened_hidden, conv2_weight, kernel_map, "kdc,cbr->kdbr")
    residual = lax.dynamic_slice_in_dim(
        owner_rows.reshape(block_count * BLK, channels), channel_start, width_out, 1
    )
    refined = jax.nn.relu(
        second * gain_second[:, None] + bias_second[:, None] + residual.T.astype(jnp.float32)
    ).astype(jnp.bfloat16)
    children = refined.reshape(width_out, block_count, 8, 8)
    partial_value = jnp.einsum(
        "oic,inoq->cnq", down_weight, children, preferred_element_type=jnp.float32
    )
    coarse = lax.psum_scatter(
        partial_value.reshape(width_out * lax.axis_size("chan"), block_count * 8).astype(
            jnp.bfloat16
        ),
        "chan",
        scatter_dimension=0,
        tiled=True,
    ).astype(jnp.float32)
    tile_values = jax.nn.relu(coarse * gain_down[:, None] + bias_down[:, None]).astype(jnp.bfloat16)
    tile_values = tile_values.reshape(width_out, block_count, 8)
    capacity = max(2, 2 * block_count // owners)
    destination = down_route[:, 0]
    onehot = (destination[:, None] == jnp.arange(owners, dtype=jnp.int32)[None, :]).astype(
        jnp.int32
    )
    earlier = jnp.sum((jnp.cumsum(onehot, axis=0) - onehot) * onehot, axis=1)
    position = destination * capacity + earlier
    selector = (
        position[None, :] == jnp.arange(owners * capacity, dtype=jnp.int32)[:, None]
    ).astype(jnp.bfloat16)
    outgoing = jnp.einsum(
        "pn,cnq->cpq", selector, tile_values, preferred_element_type=jnp.float32
    ).astype(jnp.bfloat16)
    outgoing = outgoing.reshape(width_out, owners, capacity * 8)
    arrived = lax.all_to_all(outgoing, ("brick", "sub"), split_axis=1, concat_axis=2, tiled=True)
    return arrived.reshape(1, width_out, owners * capacity * 8)


def solution(mesh):
    placed = (
        P(("groups", "brick", "chan", "sub"), None),
        P(("groups", "brick", "chan", "sub"), None),
        P(("groups", "brick", "sub"), None),
        P(("groups", "brick", "sub"), None),
        P(("groups", "brick", "sub"), None),
        P(None, "chan", None),
        P(None, "chan", None),
        P(None, "chan", None),
        P("chan"),
        P("chan"),
        P("chan"),
        P("chan"),
        P("chan"),
        P("chan"),
    )
    return jax.shard_map(
        body,
        mesh=mesh,
        in_specs=placed,
        out_specs=P(("groups", "brick", "sub"), "chan", None),
        check_vma=False,
    )
```

profile of v0, /device:TPU:0, one launch (start us, length us, event | category | flops | bytes accessed | tf_op | source)
XLA Modules:
  0.0 39.6 jit_solution(16925977249753034057)
XLA Ops:
  0.0 38.1 %encoder_level.1 = bf16[1,128,256]{2,1,0:T(8,128)(2,1)} custom-call(bf16[512,256]{1,0:T(8,128)(2,1)} %features_hbm.1, s32[1,512]{1,0:T(1,128)} %scan_order_hbm.1, s32[16,27]{1,0:T(8,128)} %kernel_map_hbm.1, s32[2,2]{1,0:T(2,128)} %halo_send_hbm.1, s32[1,16]{1,0:T(1,128)} %bitcast.11, bf16[3456,256]{1,0:T(8,128)(2,1)} %bitcast.9, bf16[3456,256]{1,0:T(8,128)(2,1)} %bitcast.10, ...), custom_call_target="tpu_custom_call" | custom-call | tf_op jit(solution)/shard_map/encoder_level/pallas_call | solution.py:477
  38.1 1.5 %copy.16 = bf16[1,128,256]{2,1,0:T(8,128)(2,1)} copy(bf16[1,128,256]{2,1,0:T(8,128)(2,1)} %encoder_level.1) | data formatting | bytes 131072
where the time goes:
time: 39.8 us; the launch traced here: 39.6 us
  Pallas kernels  38.1 us (96%)
  local copies, waits for them, and re-layouts  1.47 us (4%)
    pallas_call x1, Pallas kernels, fused(): pl.pallas_call(functools.partial(fused_kernel, axes), out_shape=jax.Shape...  38.1 us
    unnamed x1, local copies, waits for them, and re-layouts  1.47 us

commit v1 on v0

--- a/solution.py
+++ b/solution.py
@@ -89,8 +89,7 @@
     prod,
     kids_ref,
     part,
-    part_out,
-    part_in,
+    selector,
     tile_out,
     tile_in,
     w_sem,
@@ -104,8 +103,6 @@
     hid_r,
     hh_s,
     hh_r,
-    part_s,
-    part_r,
     tile_s,
     tile_r,
 ):
@@ -184,13 +181,6 @@
     for load in loads:
         load.start()
 
-    spare = conv1_w.shape[0] - taps * width
-    if spare:
-        conv1_w[pl.ds(taps * width, spare), :] = jnp.zeros((spare, channels), jnp.bfloat16)
-        conv2_w[pl.ds(taps * width, spare), :] = jnp.zeros((spare, channels), jnp.bfloat16)
-    for k in range(taps):
-        prod[k, blocks + 2 * hcap] = jnp.zeros((BLK, width), jnp.float32)
-
     for load in staged[:2]:
         load.wait()
     count = features.shape[0]
@@ -255,8 +245,30 @@
         products(ext[place].reshape(brick_blocks * BLK, channels), conv1_w, prod, place)
 
     pass_on(0)
+    spare = conv1_w.shape[0] - taps * width
+    if spare:
+        conv1_w[pl.ds(taps * width, spare), :] = jnp.zeros((spare, channels), jnp.bfloat16)
+        conv2_w[pl.ds(taps * width, spare), :] = jnp.zeros((spare, channels), jnp.bfloat16)
+    for k in range(taps):
+        prod[k, blocks + 2 * hcap] = jnp.zeros((BLK, width), jnp.float32)
+
     for load in staged[2:]:
         load.wait()
+    slots = tile_out.shape[2]
+    kids = down_w.shape[0]
+    cells = BLK // kids
+    capacity = slots // cells
+    column = lax.broadcasted_iota(jnp.int32, (1, blocks * cells), 1)
+    target_row = lax.rem(column, cells)
+    names = [down_route[0, n] for n in range(blocks)]
+    for n in range(blocks):
+        earlier = jnp.int32(0)
+        for before in range(n):
+            earlier = earlier + jnp.where(names[before] == names[n], 1, 0)
+        position = (names[n] * capacity + earlier) * cells
+        target_row = target_row + jnp.where(lax.div(column, cells) == n, position, 0)
+    slot_row = lax.broadcasted_iota(jnp.int32, (owners * slots, blocks * cells), 0)
+    selector[...] = jnp.where(slot_row == target_row, 1.0, 0.0).astype(jnp.bfloat16)
     loads[0].wait()
     for m in range(1, n_brick):
         pass_on(m)
@@ -368,8 +380,6 @@
     products(jnp.concatenate(halves, axis=1), conv2_w, prod, rim)
     second_products(group_count - 1)
     loads[1].wait()
-    kids = down_w.shape[0]
-    cells = BLK // kids
 
     def second_block(n, carry):
         second = gathered_sum(prod, kernel_map, n)
@@ -387,57 +397,32 @@
         product = jnp.dot(child, down_w[o], preferred_element_type=jnp.float32)
         partial = product if partial is None else partial + product
     part[...] = partial
-    part_copies = []
+    scaled = part[:, own_cols] * gain_down[...] + bias_down[...]
+    sides = [scaled.astype(jnp.bfloat16)]
     for j in range(1, n_chan):
         cols = pl.ds(pl.multiple_of(chan_at(j) * width, LANES), width)
-        part_out[j - 1] = part[:, cols].astype(jnp.bfloat16)
-        copy = remote(
-            part_out.at[j - 1],
-            part_in.at[j - 1],
-            part_s.at[j - 1],
-            part_r.at[j - 1],
-            device(me, chan_at(j)),
-        )
-        copy.start()
-        part_copies.append(copy)
-    pending += part_copies
-
-    slots = tile_out.shape[1]
-    capacity = slots // cells
-    column = lax.broadcasted_iota(jnp.int32, (1, blocks * cells), 1)
-    target_row = lax.rem(column, cells)
-    names = [down_route[0, n] for n in range(blocks)]
-    for n in range(blocks):
-        earlier = jnp.int32(0)
-        for before in range(n):
-            earlier = earlier + jnp.where(names[before] == names[n], 1, 0)
-        position = (names[n] * capacity + earlier) * cells
-        target_row = target_row + jnp.where(lax.div(column, cells) == n, position, 0)
-    slot_row = lax.broadcasted_iota(jnp.int32, (owners * slots, blocks * cells), 0)
-    selector = jnp.where(slot_row == target_row, 1.0, 0.0).astype(jnp.bfloat16)
-
-    coarse = part[:, own_cols]
-    for j in range(1, n_chan):
-        part_copies[j - 1].wait_recv()
-        coarse = coarse + part_in[j - 1].astype(jnp.float32)
-    tiles = jnp.maximum(coarse * gain_down[...] + bias_down[...], 0.0).astype(jnp.bfloat16)
-    outgoing = jnp.dot(selector, tiles, preferred_element_type=jnp.float32)
-    tile_out[...] = outgoing.astype(jnp.bfloat16).reshape(owners, slots, width)
+        sides.append(part[:, cols].astype(jnp.bfloat16))
+    outgoing = jnp.dot(
+        selector[...], jnp.concatenate(sides, axis=1), preferred_element_type=jnp.float32
+    ).astype(jnp.bfloat16)
+    for j in range(n_chan):
+        tile_out[j] = outgoing[:, j * width : (j + 1) * width].reshape(owners, slots, width)
     tile_copies = []
-    for i in range(1, owners):
+    for i in reversed(range(owners)):
         target = flip(me, i)
-        copy = remote(
-            tile_out.at[target],
-            tile_in.at[me],
-            tile_s.at[i - 1],
-            tile_r.at[i - 1],
-            device(target, chan),
-        )
-        copy.start()
-        tile_copies.append(copy)
-    pending += tile_copies
-    tile_in[me] = tile_out[me]
-    for copy in pending[: -len(tile_copies)]:
+        for j in range(n_chan):
+            if i or j:
+                copy = remote(
+                    tile_out.at[j, target],
+                    tile_in.at[j, me],
+                    tile_s.at[j, i],
+                    tile_r.at[j, i],
+                    device(target, chan_at(j)),
+                )
+                copy.start()
+                tile_copies.append(copy)
+    tile_in[0, me] = tile_out[0, me]
+    for copy in pending:
         copy.wait_send()
     for direction, sends in ((0, has_next), (1, has_last)):
 
@@ -449,8 +434,11 @@
 
     for copy in tile_copies:
         copy.wait_recv()
-    arrived = tile_in[...].reshape(owners * slots, width).astype(jnp.float32)
-    out[0] = arrived.T.astype(jnp.bfloat16)
+    arrived = tile_in[0].reshape(owners * slots, width).astype(jnp.float32)
+    for j in range(1, n_chan):
+        other = tile_in[j].reshape(owners * slots, width).astype(jnp.float32)
+        arrived = arrived + other * gain_down[...]
+    out[0] = jnp.maximum(arrived, 0.0).T.astype(jnp.bfloat16)
     for copy in tile_copies:
         copy.wait_send()
 
@@ -476,7 +464,7 @@
 
     return pl.pallas_call(
         functools.partial(fused_kernel, axes),
-        out_shape=jax.ShapeDtypeStruct((1, width, owners * slots), bf16),
+        out_shape=pltpu.VMEM((1, width, owners * slots), bf16),
         in_specs=[hbm] * 14,
         out_specs=vmem,
         scratch_shapes=[
@@ -501,21 +489,19 @@
             pltpu.VMEM((even_taps, blocks + 2 * hcap + 1, BLK, width), f32),
             pltpu.VMEM((wd.shape[0], blocks, cells, width), f32),
             pltpu.VMEM((blocks * cells, channels), f32),
-            pltpu.VMEM((n_chan - 1, blocks * cells, width), bf16),
-            pltpu.VMEM((n_chan - 1, blocks * cells, width), bf16),
-            pltpu.VMEM((owners, slots, width), bf16),
-            pltpu.VMEM((owners, slots, width), bf16),
+            pltpu.VMEM((owners * slots, blocks * cells), bf16),
+            pltpu.VMEM((n_chan, owners, slots, width), bf16),
+            pltpu.VMEM((n_chan, owners, slots, width), bf16),
             pltpu.SemaphoreType.DMA((2 + n_chan,)),
             *pair(owners - 1),
             *pair(n_chan - 1, owners),
             *pair(2),
             *pair(n_chan - 1, groups),
             *pair(2, n_chan),
-            *pair(n_chan - 1),
-            *pair(owners - 1),
+            *pair(n_chan, owners),
         ],
         compiler_params=pltpu.CompilerParams(
-            collective_id=0, has_side_effects=True, vmem_limit_bytes=67043328
+            collective_id=0, has_side_effects=True, vmem_limit_bytes=48 << 20
         ),
         name="encoder_level",
     )(
@@ -549,22 +535,28 @@
     return from_behind(blocks, ("brick", "sub"), step_by)
 
 
-def convolve(extended, weight, kernel_map, pattern):
+def picked(index, source):
+    chosen = jnp.arange(source.shape[0], dtype=jnp.int32)[None, :] == index[:, None]
+    flat = source.reshape(source.shape[0], -1)
+    rows = jnp.dot(chosen.astype(source.dtype), flat, preferred_element_type=jnp.float32)
+    return rows.astype(source.dtype).reshape(index.shape[0], *source.shape[1:])
+
+
+def convolve(extended, weight, kernel_map):
     block_count = kernel_map.shape[0]
-    width_out = weight.shape[1]
-    groups = weight.shape[0] // 3
-    weight_groups = weight.reshape(groups, 3, width_out, weight.shape[2])
-    index_groups = kernel_map.T.reshape(groups, 3, block_count)
-    offsets = jnp.arange(3, dtype=jnp.int32)[:, None]
-
-    def one_group(running, inputs):
-        group_weight, indices = inputs
-        product = jnp.einsum(pattern, group_weight, extended, preferred_element_type=jnp.float32)
-        return (running + jnp.sum(product[offsets, :, indices], axis=0), None)
-
-    initial = jnp.zeros((block_count, width_out, BLK), jnp.float32)
-    running, _ = lax.scan(one_group, initial, (weight_groups, index_groups))
-    return running.transpose(1, 0, 2).reshape(width_out, block_count * BLK)
+
+    def one_tap(running, inputs):
+        tap_weight, index = inputs
+        return running + jnp.einsum(
+            "brc,dc->brd",
+            picked(index, extended),
+            tap_weight,
+            preferred_element_type=jnp.float32,
+        ), None
+
+    initial = jnp.zeros((block_count, BLK, weight.shape[1]), jnp.float32)
+    running, _ = lax.scan(one_tap, initial, (weight, kernel_map.T))
+    return running
 
 
 def body(
@@ -608,34 +600,26 @@
     width_out = conv1_weight.shape[1]
     block_count = kernel_map.shape[0]
     channel_start = lax.axis_index("chan") * width_out
-    ordered = features[scan_order[0]].reshape(owners, per_owner, channels)
+    ordered = picked(scan_order[0], features).reshape(owners, per_owner, channels)
     regrouped = lax.all_to_all(ordered, ("brick", "sub"), split_axis=0, concat_axis=0, tiled=True)
     owner_rows = lax.all_gather(regrouped, "chan", axis=1, tiled=True)
     row_blocks = owner_rows.reshape(block_count, BLK, channels)
-    from_lower = neighbours(row_blocks[halo_send[0]], 1)
-    from_upper = neighbours(row_blocks[halo_send[1]], -1)
-    empty_rows = jnp.zeros((1, BLK, channels), jnp.bfloat16)
-    extended = jnp.concatenate([row_blocks, from_lower, from_upper, empty_rows], axis=0)
-    conv_first = convolve(extended, conv1_weight, kernel_map, "kdc,brc->kdbr")
-    hidden = jax.nn.relu(conv_first * gain_first[:, None] + bias_first[:, None]).astype(
-        jnp.bfloat16
-    )
-    hidden_blocks = hidden.reshape(width_out, block_count, BLK)
-    empty_cols = jnp.zeros((channels, 1, BLK), jnp.bfloat16)
-    all_channels = lax.all_gather(hidden_blocks, "chan", axis=0, tiled=True)
-    lower_cols = neighbours(all_channels[:, halo_send[0]], 1)
-    upper_cols = neighbours(all_channels[:, halo_send[1]], -1)
-    widened_hidden = jnp.concatenate([all_channels, lower_cols, upper_cols, empty_cols], axis=1)
-    second = convolve(widened_hidden, conv2_weight, kernel_map, "kdc,cbr->kdbr")
-    residual = lax.dynamic_slice_in_dim(
-        owner_rows.reshape(block_count * BLK, channels), channel_start, width_out, 1
-    )
-    refined = jax.nn.relu(
-        second * gain_second[:, None] + bias_second[:, None] + residual.T.astype(jnp.float32)
-    ).astype(jnp.bfloat16)
-    children = refined.reshape(width_out, block_count, 8, 8)
+
+    def extend(own):
+        from_lower = neighbours(picked(halo_send[0], own), 1)
+        from_upper = neighbours(picked(halo_send[1], own), -1)
+        empty = jnp.zeros((1, BLK, channels), jnp.bfloat16)
+        return jnp.concatenate([own, from_lower, from_upper, empty], axis=0)
+
+    conv_first = convolve(extend(row_blocks), conv1_weight, kernel_map)
+    hidden = jax.nn.relu(conv_first * gain_first + bias_first).astype(jnp.bfloat16)
+    all_channels = lax.all_gather(hidden, "chan", axis=2, tiled=True)
+    second = convolve(extend(all_channels), conv2_weight, kernel_map)
+    residual = lax.dynamic_slice_in_dim(row_blocks, channel_start, width_out, 2)
+    refined = jax.nn.relu(second * gain_second + bias_second + residual.astype(jnp.float32))
+    children = refined.astype(jnp.bfloat16).reshape(block_count, 8, 8, width_out)
     partial_value = jnp.einsum(
-        "oic,inoq->cnq", down_weight, children, preferred_element_type=jnp.float32
+        "oic,noqi->cnq", down_weight, children, preferred_element_type=jnp.float32
     )
     coarse = lax.psum_scatter(
         partial_value.reshape(width_out * lax.axis_size("chan"), block_count * 8).astype(
@@ -649,11 +633,9 @@
     tile_values = tile_values.reshape(width_out, block_count, 8)
     capacity = max(2, 2 * block_count // owners)
     destination = down_route[:, 0]
-    onehot = (destination[:, None] == jnp.arange(owners, dtype=jnp.int32)[None, :]).astype(
-        jnp.int32
-    )
-    earlier = jnp.sum((jnp.cumsum(onehot, axis=0) - onehot) * onehot, axis=1)
-    position = destination * capacity + earlier
+    number = jnp.arange(block_count, dtype=jnp.int32)
+    alike = (destination[:, None] == destination[None, :]) & (number[:, None] > number[None, :])
+    position = destination * capacity + jnp.sum(alike.astype(jnp.int32), axis=1)
     selector = (
         position[None, :] == jnp.arange(owners * capacity, dtype=jnp.int32)[:, None]
     ).astype(jnp.bfloat16)

time: 39.8 us -> 49.5 us (1.24)
  local copies, waits for them, and re-layouts: 1.47 us -> 12.2 us
  Pallas kernels: 38.1 us -> 36.9 us
    unnamed x1 -> x29, local copies, waits for them, and re-layouts: 1.47 us -> 12.2 us
    pallas_call x1, Pallas kernels: 38.1 us -> 36.9 us  [fused(): pl.pallas_call(functools.partial(fused_kernel, axes), out_shape=pltpu.VME...]
where the time goes in v1:
time: 49.5 us; the launch traced here: 49.1 us
  Pallas kernels  36.9 us (75%)
  local copies, waits for them, and re-layouts  12.2 us (25%)
    pallas_call x1, Pallas kernels, fused(): pl.pallas_call(functools.partial(fused_kernel, axes), out_shape=pltpu.VME...  36.9 us
    unnamed x29, local copies, waits for them, and re-layouts  12.2 us

profile of v1, /device:TPU:0, one launch (start us, length us, event | category | flops | bytes accessed | tf_op | source)
XLA Modules:
  0.0 49.1 jit_solution(8642525127827301335)
XLA Ops:
  0.0 0.0 copy-start
  0.0 1.5 %copy-done = bf16[27,128,256]{2,1,0:T(8,128)(2,1)S(1)} copy-done((bf16[27,128,256]{2,1,0:T(8,128)(2,1)S(1)}, bf16[27,128,256]{2,1,0:T(8,128)(2,1)}, u32[]{:S(2)}) %copy-start) | copy-done | bytes 1769496
  1.5 0.0 copy-start.1
  1.5 1.5 %copy-done.1 = bf16[27,128,256]{2,1,0:T(8,128)(2,1)S(1)} copy-done((bf16[27,128,256]{2,1,0:T(8,128)(2,1)S(1)}, bf16[27,128,256]{2,1,0:T(8,128)(2,1)}, u32[]{:S(2)}) %copy-start.1) | copy-done | bytes 1769496
  3.0 0.0 copy-start.2
  3.0 1.0 %copy-done.2 = bf16[8,128,256]{2,1,0:T(8,128)(2,1)S(1)} copy-done((bf16[8,128,256]{2,1,0:T(8,128)(2,1)S(1)}, bf16[8,128,256]{2,1,0:T(8,128)(2,1)}, u32[]{:S(2)}) %copy-start.2) | copy-done | bytes 524312
  4.0 0.0 copy-start.3
  4.0 0.9 %copy-done.3 = bf16[512,256]{1,0:T(8,128)(2,1)S(1)} copy-done((bf16[512,256]{1,0:T(8,128)(2,1)S(1)}, bf16[512,256]{1,0:T(8,128)(2,1)}, u32[]{:S(2)}) %copy-start.3) | copy-done | bytes 262168
  4.9 0.0 copy-start.4
  4.9 0.7 %copy-done.4 = s32[16,27]{1,0:T(8,128)S(1)} copy-done((s32[16,27]{1,0:T(8,128)S(1)}, s32[16,27]{1,0:T(8,128)}, u32[]{:S(2)}) %copy-start.4) | copy-done | bytes 1752
  5.6 0.0 copy-start.5
  5.6 0.7 %copy-done.5 = s32[1,512]{1,0:T(1,128)S(1)} copy-done((s32[1,512]{1,0:T(1,128)S(1)}, s32[1,512]{1,0:T(1,128)}, u32[]{:S(2)}) %copy-start.5) | copy-done | bytes 2072
  6.3 0.0 copy-start.6
  6.3 0.7 %copy-done.6 = s32[2,2]{1,0:T(2,128)S(1)} copy-done((s32[2,2]{1,0:T(2,128)S(1)}, s32[2,2]{1,0:T(2,128)}, u32[]{:S(2)}) %copy-start.6) | copy-done | bytes 40
  7.0 0.0 copy-start.7
  7.0 0.7 %copy-done.7 = s32[16,1]{0,1:T(1,128)S(1)} copy-done((s32[16,1]{0,1:T(1,128)S(1)}, s32[16,1]{0,1:T(1,128)}, u32[]{:S(2)}) %copy-start.7) | copy-done | bytes 88
  7.7 0.7 %copy-done.8 = f32[128]{0:T(128)S(1)} copy-done((f32[128]{0:T(128)S(1)}, f32[128]{0:T(128)}, u32[]{:S(2)}) %copy-start.8) | copy-done | bytes 536
  8.3 0.7 %copy-done.9 = f32[128]{0:T(128)S(1)} copy-done((f32[128]{0:T(128)S(1)}, f32[128]{0:T(128)}, u32[]{:S(2)}) %copy-start.9) | copy-done | bytes 536
  9.0 0.7 %copy-done.10 = f32[128]{0:T(128)S(1)} copy-done((f32[128]{0:T(128)S(1)}, f32[128]{0:T(128)}, u32[]{:S(2)}) %copy-start.10) | copy-done | bytes 536
  9.6 0.7 %copy-done.11 = f32[128]{0:T(128)S(1)} copy-done((f32[128]{0:T(128)S(1)}, f32[128]{0:T(128)}, u32[]{:S(2)}) %copy-start.11) | copy-done | bytes 536
  10.3 0.7 %copy-done.12 = f32[128]{0:T(128)S(1)} copy-done((f32[128]{0:T(128)S(1)}, f32[128]{0:T(128)}, u32[]{:S(2)}) %copy-start.12) | copy-done | bytes 536
  10.9 0.7 %copy-done.13 = f32[128]{0:T(128)S(1)} copy-done((f32[128]{0:T(128)S(1)}, f32[128]{0:T(128)}, u32[]{:S(2)}) %copy-start.13) | copy-done | bytes 536
  11.6 36.9 %encoder_level.1 = bf16[1,128,256]{2,1,0:T(8,128)(2,1)S(1)} custom-call(bf16[512,256]{1,0:T(8,128)(2,1)S(1)} %copy-done.3, s32[1,512]{1,0:T(1,128)S(1)} %copy-done.5, s32[16,27]{1,0:T(8,128)S(1)} %copy-done.4, s32[2,2]{1,0:T(2,128)S(1)} %copy-done.6, s32[1,16]{1,0:T(1,128)S(1)} %bitcast.11, bf16[3456,256]{1,0:T(8,128)(2,1)S(1)} %bitcast.9, ...), custom_call_target="tpu_custom_call" | custom-call | tf_op jit(solution)/shard_map/encoder_level/pallas_call | solution.py:465
  48.5 0.6 %copy.16 = bf16[1,128,256]{2,1,0:T(8,128)(2,1)} copy(bf16[1,128,256]{2,1,0:T(8,128)(2,1)S(1)} %encoder_level.1) | data formatting | bytes 131072
  (6 shorter events, 0.0 us)
Async XLA Ops:
  0.0 1.5 %copy-start = (bf16[27,128,256]{2,1,0:T(8,128)(2,1)S(1)}, bf16[27,128,256]{2,1,0:T(8,128)(2,1)}, u32[]{:S(2)}) copy-start(bf16[27,128,256]{2,1,0:T(8,128)(2,1)} %param.19) | copy-start | bytes 5308420
  1.5 1.5 %copy-start.1 = (bf16[27,128,256]{2,1,0:T(8,128)(2,1)S(1)}, bf16[27,128,256]{2,1,0:T(8,128)(2,1)}, u32[]{:S(2)}) copy-start(bf16[27,128,256]{2,1,0:T(8,128)(2,1)} %param.20) | copy-start | bytes 5308420
  3.0 1.0 %copy-start.2 = (bf16[8,128,256]{2,1,0:T(8,128)(2,1)S(1)}, bf16[8,128,256]{2,1,0:T(8,128)(2,1)}, u32[]{:S(2)}) copy-start(bf16[8,128,256]{2,1,0:T(8,128)(2,1)} %down_hbm.1) | copy-start | bytes 1572868
  4.0 0.9 %copy-start.3 = (bf16[512,256]{1,0:T(8,128)(2,1)S(1)}, bf16[512,256]{1,0:T(8,128)(2,1)}, u32[]{:S(2)}) copy-start(bf16[512,256]{1,0:T(8,128)(2,1)} %features_hbm.1) | copy-start | bytes 786436
  4.9 0.7 %copy-start.4 = (s32[16,27]{1,0:T(8,128)S(1)}, s32[16,27]{1,0:T(8,128)}, u32[]{:S(2)}) copy-start(s32[16,27]{1,0:T(8,128)} %kernel_map_hbm.1) | copy-start | bytes 5188
  5.6 0.7 %copy-start.5 = (s32[1,512]{1,0:T(1,128)S(1)}, s32[1,512]{1,0:T(1,128)}, u32[]{:S(2)}) copy-start(s32[1,512]{1,0:T(1,128)} %scan_order_hbm.1) | copy-start | bytes 6148
  6.3 0.7 %copy-start.6 = (s32[2,2]{1,0:T(2,128)S(1)}, s32[2,2]{1,0:T(2,128)}, u32[]{:S(2)}) copy-start(s32[2,2]{1,0:T(2,128)} %halo_send_hbm.1) | copy-start | bytes 52
  7.0 0.7 %copy-start.7 = (s32[16,1]{0,1:T(1,128)S(1)}, s32[16,1]{0,1:T(1,128)}, u32[]{:S(2)}) copy-start(s32[16,1]{0,1:T(1,128)} %param.18) | copy-start | bytes 196
  7.7 0.7 %copy-start.8 = (f32[128]{0:T(128)S(1)}, f32[128]{0:T(128)}, u32[]{:S(2)}) copy-start(f32[128]{0:T(128)} %param.22) | copy-start | bytes 1540
  8.3 0.7 %copy-start.9 = (f32[128]{0:T(128)S(1)}, f32[128]{0:T(128)}, u32[]{:S(2)}) copy-start(f32[128]{0:T(128)} %param.23) | copy-start | bytes 1540
  9.0 0.7 %copy-start.10 = (f32[128]{0:T(128)S(1)}, f32[128]{0:T(128)}, u32[]{:S(2)}) copy-start(f32[128]{0:T(128)} %param.24) | copy-start | bytes 1540
  9.6 0.7 %copy-start.11 = (f32[128]{0:T(128)S(1)}, f32[128]{0:T(128)}, u32[]{:S(2)}) copy-start(f32[128]{0:T(128)} %param.25) | copy-start | bytes 1540
  10.3 0.7 %copy-start.12 = (f32[128]{0:T(128)S(1)}, f32[128]{0:T(128)}, u32[]{:S(2)}) copy-start(f32[128]{0:T(128)} %param.26) | copy-start | bytes 1540
  10.9 0.7 %copy-start.13 = (f32[128]{0:T(128)S(1)}, f32[128]{0:T(128)}, u32[]{:S(2)}) copy-start(f32[128]{0:T(128)} %param.27) | copy-start | bytes 1540

commit v2 on v1

--- a/solution.py
+++ b/solution.py
@@ -272,8 +272,9 @@
     loads[0].wait()
     for m in range(1, n_brick):
         pass_on(m)
-        collect(m - 1)
-        multiply(m - 1)
+    for m in range(n_brick - 1):
+        collect(m)
+        multiply(m)
     collect(n_brick - 1)
     pending += [copy for copies in forwards for copy in copies]
 
@@ -338,7 +339,7 @@
             hid_own[n] = first_hidden(n)
             return carry
 
-        lax.fori_loop(g * group, (g + 1) * group, first_block, 0)
+        lax.fori_loop(g * group, (g + 1) * group, first_block, 0, unroll=2)
         place = pl.ds(g * group, group)
         for j in range(1, n_chan):
             copy = remote(
@@ -390,7 +391,7 @@
             kids_ref[o, n] = refined[o]
         return carry
 
-    lax.fori_loop(0, blocks, second_block, 0)
+    lax.fori_loop(0, blocks, second_block, 0, unroll=4)
     partial = None
     for o in range(kids):
         child = kids_ref[o].reshape(blocks * cells, width).astype(jnp.bfloat16)
@@ -501,7 +502,7 @@
             *pair(n_chan, owners),
         ],
         compiler_params=pltpu.CompilerParams(
-            collective_id=0, has_side_effects=True, vmem_limit_bytes=48 << 20
+            collective_id=0, has_side_effects=True, vmem_limit_bytes=66977792
         ),
         name="encoder_level",
     )(

time: 49.5 us -> 36.5 us (0.74)
  local copies, waits for them, and re-layouts: 12.2 us -> 0.63 us
  Pallas kernels: 36.9 us -> 35.7 us
    unnamed x29 -> x1, local copies, waits for them, and re-layouts: 12.2 us -> 0.63 us
    pallas_call x1, Pallas kernels: 36.9 us -> 35.7 us  [fused(): pl.pallas_call(functools.partial(fused_kernel, axes), out_shape=pltpu.VME...]
where the time goes in v2:
time: 36.5 us; the launch traced here: 36.4 us
  Pallas kernels  35.7 us (98%)
  local copies, waits for them, and re-layouts  0.63 us (2%)
    pallas_call x1, Pallas kernels, fused(): pl.pallas_call(functools.partial(fused_kernel, axes), out_shape=pltpu.VME...  35.7 us

profile of v2, /device:TPU:0, one launch (start us, length us, event | category | flops | bytes accessed | tf_op | source)
XLA Modules:
  0.0 36.4 jit_solution(5184322053770875298)
XLA Ops:
  0.0 35.7 %encoder_level.1 = bf16[1,128,256]{2,1,0:T(8,128)(2,1)S(1)} custom-call(bf16[512,256]{1,0:T(8,128)(2,1)} %features_hbm.1, s32[1,512]{1,0:T(1,128)} %scan_order_hbm.1, s32[16,27]{1,0:T(8,128)} %kernel_map_hbm.1, s32[2,2]{1,0:T(2,128)} %halo_send_hbm.1, s32[1,16]{1,0:T(1,128)} %bitcast.11, bf16[3456,256]{1,0:T(8,128)(2,1)} %bitcast.9, ...), custom_call_target="tpu_custom_call" | custom-call | tf_op jit(solution)/shard_map/encoder_level/pallas_call | solution.py:466
  35.7 0.6 %copy.16 = bf16[1,128,256]{2,1,0:T(8,128)(2,1)} copy(bf16[1,128,256]{2,1,0:T(8,128)(2,1)S(1)} %encoder_level.1) | data formatting | bytes 131072

commit v3 on v2

--- a/solution.py
+++ b/solution.py
@@ -408,20 +408,24 @@
     ).astype(jnp.bfloat16)
     for j in range(n_chan):
         tile_out[j] = outgoing[:, j * width : (j + 1) * width].reshape(owners, slots, width)
-    tile_copies = []
-    for i in reversed(range(owners)):
-        target = flip(me, i)
-        for j in range(n_chan):
-            if i or j:
-                copy = remote(
-                    tile_out.at[j, target],
-                    tile_in.at[j, me],
-                    tile_s.at[j, i],
-                    tile_r.at[j, i],
-                    device(target, chan_at(j)),
-                )
-                copy.start()
-                tile_copies.append(copy)
+    def tile_copy(j, target, source):
+        return remote(
+            tile_out.at[j, target],
+            tile_in.at[j, source],
+            tile_s.at[j, target],
+            tile_r.at[j, source],
+            device(target, chan_at(j)),
+        )
+
+    def tile_copies(act):
+        for other in [*range(n_sub), *reversed(range(n_sub, owners))]:
+            for j in reversed(range(n_chan)):
+                if j:
+                    act(j, other)
+                else:
+                    pl.when(me != other)(functools.partial(act, j, other))
+
+    tile_copies(lambda j, other: tile_copy(j, other, me).start())
     tile_in[0, me] = tile_out[0, me]
     for copy in pending:
         copy.wait_send()
@@ -433,15 +437,13 @@
             for copy in hid_halo_copies(direction):
                 copy.wait_send()
 
-    for copy in tile_copies:
-        copy.wait_recv()
+    tile_copies(lambda j, other: tile_copy(j, other, other).wait_recv())
     arrived = tile_in[0].reshape(owners * slots, width).astype(jnp.float32)
     for j in range(1, n_chan):
         other = tile_in[j].reshape(owners * slots, width).astype(jnp.float32)
         arrived = arrived + other * gain_down[...]
     out[0] = jnp.maximum(arrived, 0.0).T.astype(jnp.bfloat16)
-    for copy in tile_copies:
-        copy.wait_send()
+    tile_copies(lambda j, other: tile_copy(j, other, other).wait_send())
 
 
 def fused(axes, features, scan_order, kernel_map, halo_send, down_route, w1, w2, wd, *scales):

time: 36.5 us -> 35.8 us (0.981)
  Pallas kernels: 35.7 us -> 35 us
    pallas_call x1, Pallas kernels: 35.7 us -> 35 us  [fused(): pl.pallas_call(functools.partial(fused_kernel, axes), out_shape=pltpu.VME...]
where the time goes in v3:
time: 35.8 us; the launch traced here: 35.6 us
  Pallas kernels  35 us (98%)
  local copies, waits for them, and re-layouts  0.63 us (2%)
    pallas_call x1, Pallas kernels, fused(): pl.pallas_call(functools.partial(fused_kernel, axes), out_shape=pltpu.VME...  35 us

profile of v3, /device:TPU:0, one launch (start us, length us, event | category | flops | bytes accessed | tf_op | source)
XLA Modules:
  0.0 35.6 jit_solution(15426058315420549296)
XLA Ops:
  0.0 35.0 %encoder_level.1 = bf16[1,128,256]{2,1,0:T(8,128)(2,1)S(1)} custom-call(bf16[512,256]{1,0:T(8,128)(2,1)} %features_hbm.1, s32[1,512]{1,0:T(1,128)} %scan_order_hbm.1, s32[16,27]{1,0:T(8,128)} %kernel_map_hbm.1, s32[2,2]{1,0:T(2,128)} %halo_send_hbm.1, s32[1,16]{1,0:T(1,128)} %bitcast.11, bf16[3456,256]{1,0:T(8,128)(2,1)} %bitcast.9, ...), custom_call_target="tpu_custom_call" | custom-call | tf_op jit(solution)/shard_map/encoder_level/pallas_call | solution.py:468
  35.0 0.6 %copy.16 = bf16[1,128,256]{2,1,0:T(8,128)(2,1)} copy(bf16[1,128,256]{2,1,0:T(8,128)(2,1)S(1)} %encoder_level.1) | data formatting | bytes 131072

commit v4 on v3

--- a/solution.py
+++ b/solution.py
@@ -88,7 +88,6 @@
     hid_halo_in,
     prod,
     kids_ref,
-    part,
     selector,
     tile_out,
     tile_in,
@@ -173,9 +172,8 @@
             pltpu.make_async_copy(conv2_hbm.at[:, cols_from(j)], target, w_sem.at[2 + j])
         )
     barrier = pltpu.get_barrier_semaphore()
-    partners = [device(flip(me, i), chan) for i in range(1, owners)]
+    partners = [device(flip(me, i), chan) for i in reversed(range(1, owners))]
     partners += [device(me, chan_at(j)) for j in range(1, n_chan)]
-    partners += [device(owner_at(d), chan_at(j)) for j in range(1, n_chan) for d in (1, -1)]
     for partner in partners:
         pl.semaphore_signal(barrier, inc=1, device_id=partner, device_id_type=MESH)
     for load in loads:
@@ -393,40 +391,55 @@
 
     lax.fori_loop(0, blocks, second_block, 0, unroll=4)
     partial = None
-    for o in range(kids):
-        child = kids_ref[o].reshape(blocks * cells, width).astype(jnp.bfloat16)
-        product = jnp.dot(child, down_w[o], preferred_element_type=jnp.float32)
+    for o in range(0, kids, 2):
+        child = jnp.concatenate(
+            [kids_ref[o + h].reshape(blocks * cells, width) for h in range(2)], axis=1
+        ).astype(jnp.bfloat16)
+        weight = down_w[o : o + 2].reshape(2 * width, channels)
+        product = jnp.dot(child, weight, preferred_element_type=jnp.float32)
         partial = product if partial is None else partial + product
-    part[...] = partial
-    scaled = part[:, own_cols] * gain_down[...] + bias_down[...]
-    sides = [scaled.astype(jnp.bfloat16)]
-    for j in range(1, n_chan):
-        cols = pl.ds(pl.multiple_of(chan_at(j) * width, LANES), width)
-        sides.append(part[:, cols].astype(jnp.bfloat16))
-    outgoing = jnp.dot(
-        selector[...], jnp.concatenate(sides, axis=1), preferred_element_type=jnp.float32
-    ).astype(jnp.bfloat16)
-    for j in range(n_chan):
-        tile_out[j] = outgoing[:, j * width : (j + 1) * width].reshape(owners, slots, width)
-    def tile_copy(j, target, source):
-        return remote(
-            tile_out.at[j, target],
-            tile_in.at[j, source],
-            tile_s.at[j, target],
-            tile_r.at[j, source],
-            device(target, chan_at(j)),
-        )
-
-    def tile_copies(act):
-        for other in [*range(n_sub), *reversed(range(n_sub, owners))]:
-            for j in reversed(range(n_chan)):
-                if j:
-                    act(j, other)
+    mine = [chan == c for c in range(n_chan)]
+    scale = jnp.concatenate([jnp.where(own, gain_down[...], 1.0) for own in mine], axis=1)
+    shift = jnp.concatenate([jnp.where(own, bias_down[...], 0.0) for own in mine], axis=1)
+    sides = (partial * scale + shift).astype(jnp.bfloat16)
+    outgoing = jnp.dot(selector[...], sides, preferred_element_type=jnp.float32)
+    for c in range(n_chan):
+        half = outgoing[:, c * width : (c + 1) * width].astype(jnp.bfloat16)
+        tile_out[c] = half.reshape(owners, slots, width)
+
+    def send_tile(c, target):
+        side = lax.rem(c - chan + n_chan, n_chan)
+        copy = remote(
+            tile_out.at[c, target],
+            tile_in.at[side, me],
+            tile_s.at[side, target],
+            tile_r.at[side, me],
+            device(target, c),
+        )
+        pl.when(jnp.logical_or(me != target, chan != c))(copy.start)
+
+    def tiles(act):
+        for other in range(owners):
+            for side in range(n_chan):
+                copy = remote(
+                    tile_out.at[side, other],
+                    tile_in.at[side, other],
+                    tile_s.at[side, other],
+                    tile_r.at[side, other],
+                    device(other, chan_at(side)),
+                )
+                if side:
+                    act(copy)
                 else:
-                    pl.when(me != other)(functools.partial(act, j, other))
-
-    tile_copies(lambda j, other: tile_copy(j, other, me).start())
-    tile_in[0, me] = tile_out[0, me]
+                    pl.when(me != other)(functools.partial(act, copy))
+
+    for c in range(n_chan):
+        for target in range(n_sub):
+            send_tile(c, target)
+    for target in reversed(range(n_sub, owners)):
+        for c in range(n_chan):
+            send_tile(c, target)
+    tile_in[0, me] = tile_out[chan, me]
     for copy in pending:
         copy.wait_send()
     for direction, sends in ((0, has_next), (1, has_last)):
@@ -437,13 +450,13 @@
             for copy in hid_halo_copies(direction):
                 copy.wait_send()
 
-    tile_copies(lambda j, other: tile_copy(j, other, other).wait_recv())
+    tiles(lambda copy: copy.wait_recv())
     arrived = tile_in[0].reshape(owners * slots, width).astype(jnp.float32)
     for j in range(1, n_chan):
         other = tile_in[j].reshape(owners * slots, width).astype(jnp.float32)
         arrived = arrived + other * gain_down[...]
     out[0] = jnp.maximum(arrived, 0.0).T.astype(jnp.bfloat16)
-    tile_copies(lambda j, other: tile_copy(j, other, other).wait_send())
+    tiles(lambda copy: copy.wait_send())
 
 
 def fused(axes, features, scan_order, kernel_map, halo_send, down_route, w1, w2, wd, *scales):
@@ -491,7 +504,6 @@
             pltpu.VMEM((2, n_chan, hcap, BLK, width), bf16),
             pltpu.VMEM((even_taps, blocks + 2 * hcap + 1, BLK, width), f32),
             pltpu.VMEM((wd.shape[0], blocks, cells, width), f32),
-            pltpu.VMEM((blocks * cells, channels), f32),
             pltpu.VMEM((owners * slots, blocks * cells), bf16),
             pltpu.VMEM((n_chan, owners, slots, width), bf16),
             pltpu.VMEM((n_chan, owners, slots, width), bf16),

time: 35.8 us -> 35.4 us (0.989)
  Pallas kernels: 35 us -> 34.6 us
    pallas_call x1, Pallas kernels: 35 us -> 34.6 us  [fused(): pl.pallas_call(functools.partial(fused_kernel, axes), out_shape=pltpu.VME...]
where the time goes in v4:
time: 35.4 us; the launch traced here: 35.2 us
  Pallas kernels  34.6 us (98%)
  local copies, waits for them, and re-layouts  0.63 us (2%)
    pallas_call x1, Pallas kernels, fused(): pl.pallas_call(functools.partial(fused_kernel, axes), out_shape=pltpu.VME...  34.6 us

profile of v4, /device:TPU:0, one launch (start us, length us, event | category | flops | bytes accessed | tf_op | source)
XLA Modules:
  0.0 35.2 jit_solution(1564060378280447490)
XLA Ops:
  0.0 34.6 %encoder_level.1 = bf16[1,128,256]{2,1,0:T(8,128)(2,1)S(1)} custom-call(bf16[512,256]{1,0:T(8,128)(2,1)} %features_hbm.1, s32[1,512]{1,0:T(1,128)} %scan_order_hbm.1, s32[16,27]{1,0:T(8,128)} %kernel_map_hbm.1, s32[2,2]{1,0:T(2,128)} %halo_send_hbm.1, s32[1,16]{1,0:T(1,128)} %bitcast.11, bf16[3456,256]{1,0:T(8,128)(2,1)} %bitcast.9, ...), custom_call_target="tpu_custom_call" | custom-call | tf_op jit(solution)/shard_map/encoder_level/pallas_call | solution.py:481
  34.6 0.6 %copy.16 = bf16[1,128,256]{2,1,0:T(8,128)(2,1)} copy(bf16[1,128,256]{2,1,0:T(8,128)(2,1)S(1)} %encoder_level.1) | data formatting | bytes 131072

commit v5 on v4

--- a/solution.py
+++ b/solution.py
@@ -287,7 +287,7 @@
             device(owner_at(1 if direction == 0 else -1), chan),
         )
 
-    for direction, sends in ((0, has_next), (1, has_last)):
+    for direction, sends in ((1, has_last), (0, has_next)):
         for j in range(hcap):
             halo_out[direction, j] = ext[halo_send[direction, j]]
         pl.when(sends)(lambda direction=direction: halo_copies(direction).start())
@@ -321,7 +321,7 @@
             for j in range(n_chan)
         ]
 
-    for direction, sends in ((0, has_next), (1, has_last)):
+    for direction, sends in ((1, has_last), (0, has_next)):
         for j in range(hcap):
             hid_halo_out[direction, j] = first_hidden(halo_send[direction, j])
 
@@ -402,10 +402,12 @@
     scale = jnp.concatenate([jnp.where(own, gain_down[...], 1.0) for own in mine], axis=1)
     shift = jnp.concatenate([jnp.where(own, bias_down[...], 0.0) for own in mine], axis=1)
     sides = (partial * scale + shift).astype(jnp.bfloat16)
-    outgoing = jnp.dot(selector[...], sides, preferred_element_type=jnp.float32)
-    for c in range(n_chan):
-        half = outgoing[:, c * width : (c + 1) * width].astype(jnp.bfloat16)
-        tile_out[c] = half.reshape(owners, slots, width)
+    def pack_tiles(first, last):
+        chosen = selector[first * slots : last * slots, :]
+        outgoing = jnp.dot(chosen, sides, preferred_element_type=jnp.float32)
+        for c in range(n_chan):
+            half = outgoing[:, c * width : (c + 1) * width].astype(jnp.bfloat16)
+            tile_out[c, first:last] = half.reshape(last - first, slots, width)
 
     def send_tile(c, target):
         side = lax.rem(c - chan + n_chan, n_chan)
@@ -433,9 +435,11 @@
                 else:
                     pl.when(me != other)(functools.partial(act, copy))
 
+    pack_tiles(0, n_sub)
     for c in range(n_chan):
         for target in range(n_sub):
             send_tile(c, target)
+    pack_tiles(n_sub, owners)
     for target in reversed(range(n_sub, owners)):
         for c in range(n_chan):
             send_tile(c, target)

time: 35.4 us -> 35.2 us (level)
  no operation moved by 1% of the time
where the time goes in v5:
time: 35.2 us; the launch traced here: 35 us
  Pallas kernels  34.4 us (98%)
  local copies, waits for them, and re-layouts  0.63 us (2%)
    pallas_call x1, Pallas kernels, fused(): pl.pallas_call(functools.partial(fused_kernel, axes), out_shape=pltpu.VME...  34.4 us

profile of v5, /device:TPU:0, one launch (start us, length us, event | category | flops | bytes accessed | tf_op | source)
XLA Modules:
  0.0 35.0 jit_solution(5719317613602142982)
XLA Ops:
  0.0 34.4 %encoder_level.1 = bf16[1,128,256]{2,1,0:T(8,128)(2,1)S(1)} custom-call(bf16[512,256]{1,0:T(8,128)(2,1)} %features_hbm.1, s32[1,512]{1,0:T(1,128)} %scan_order_hbm.1, s32[16,27]{1,0:T(8,128)} %kernel_map_hbm.1, s32[2,2]{1,0:T(2,128)} %halo_send_hbm.1, s32[1,16]{1,0:T(1,128)} %bitcast.11, bf16[3456,256]{1,0:T(8,128)(2,1)} %bitcast.9, ...), custom_call_target="tpu_custom_call" | custom-call | tf_op jit(solution)/shard_map/encoder_level/pallas_call | solution.py:485
  34.4 0.6 %copy.16 = bf16[1,128,256]{2,1,0:T(8,128)(2,1)} copy(bf16[1,128,256]{2,1,0:T(8,128)(2,1)S(1)} %encoder_level.1) | data formatting | bytes 131072

commit v6 on v5

--- a/solution.py
+++ b/solution.py
@@ -389,7 +389,7 @@
             kids_ref[o, n] = refined[o]
         return carry
 
-    lax.fori_loop(0, blocks, second_block, 0, unroll=4)
+    lax.fori_loop(0, blocks, second_block, 0, unroll=8)
     partial = None
     for o in range(0, kids, 2):
         child = jnp.concatenate(
@@ -420,8 +420,8 @@
         )
         pl.when(jnp.logical_or(me != target, chan != c))(copy.start)
 
-    def tiles(act):
-        for other in range(owners):
+    def tiles(act, others):
+        for other in others:
             for side in range(n_chan):
                 copy = remote(
                     tile_out.at[side, other],
@@ -454,13 +454,18 @@
             for copy in hid_halo_copies(direction):
                 copy.wait_send()
 
-    tiles(lambda copy: copy.wait_recv())
-    arrived = tile_in[0].reshape(owners * slots, width).astype(jnp.float32)
-    for j in range(1, n_chan):
-        other = tile_in[j].reshape(owners * slots, width).astype(jnp.float32)
-        arrived = arrived + other * gain_down[...]
-    out[0] = jnp.maximum(arrived, 0.0).T.astype(jnp.bfloat16)
-    tiles(lambda copy: copy.wait_send())
+    together = max(1, LANES // slots)
+    for first in range(0, owners, together):
+        sources = range(first, min(first + together, owners))
+        tiles(lambda copy: copy.wait_recv(), sources)
+        group = pl.ds(first, len(sources))
+        arrived = tile_in[0, group].reshape(len(sources) * slots, width).astype(jnp.float32)
+        for j in range(1, n_chan):
+            other = tile_in[j, group].reshape(len(sources) * slots, width).astype(jnp.float32)
+            arrived = arrived + other * gain_down[...]
+        columns = pl.ds(first * slots, len(sources) * slots)
+        out[0, :, columns] = jnp.maximum(arrived, 0.0).T.astype(jnp.bfloat16)
+    tiles(lambda copy: copy.wait_send(), range(owners))
 
 
 def fused(axes, features, scan_order, kernel_map, halo_send, down_route, w1, w2, wd, *scales):

time: 35.2 us -> 35.3 us (level)
  no operation moved by 1% of the time
where the time goes in v6:
time: 35.3 us; the launch traced here: 35.1 us
  Pallas kernels  34.5 us (98%)
  local copies, waits for them, and re-layouts  0.63 us (2%)
    pallas_call x1, Pallas kernels, fused(): pl.pallas_call(functools.partial(fused_kernel, axes), out_shape=pltpu.VME...  34.5 us

profile of v6, /device:TPU:0, one launch (start us, length us, event | category | flops | bytes accessed | tf_op | source)
XLA Modules:
  0.0 35.1 jit_solution(3479736994676847376)
XLA Ops:
  0.0 34.5 %encoder_level.1 = bf16[1,128,256]{2,1,0:T(8,128)(2,1)S(1)} custom-call(bf16[512,256]{1,0:T(8,128)(2,1)} %features_hbm.1, s32[1,512]{1,0:T(1,128)} %scan_order_hbm.1, s32[16,27]{1,0:T(8,128)} %kernel_map_hbm.1, s32[2,2]{1,0:T(2,128)} %halo_send_hbm.1, s32[1,16]{1,0:T(1,128)} %bitcast.11, bf16[3456,256]{1,0:T(8,128)(2,1)} %bitcast.9, ...), custom_call_target="tpu_custom_call" | custom-call | tf_op jit(solution)/shard_map/encoder_level/pallas_call | solution.py:490
  34.5 0.6 %copy.16 = bf16[1,128,256]{2,1,0:T(8,128)(2,1)} copy(bf16[1,128,256]{2,1,0:T(8,128)(2,1)S(1)} %encoder_level.1) | data formatting | bytes 131072

commit v7 on v5

--- a/solution.py
+++ b/solution.py
@@ -321,7 +321,7 @@
             for j in range(n_chan)
         ]
 
-    for direction, sends in ((1, has_last), (0, has_next)):
+    def send_hidden_rim(direction, sends):
         for j in range(hcap):
             hid_halo_out[direction, j] = first_hidden(halo_send[direction, j])
 
@@ -330,6 +330,7 @@
             for copy in hid_halo_copies(direction):
                 copy.start()
 
+    send_hidden_rim(1, has_last)
     hid_copies = []
     for g in range(group_count):
 
@@ -349,6 +350,8 @@
             )
             copy.start()
             hid_copies.append(copy)
+        if g == 0:
+            send_hidden_rim(0, has_next)
     pending += hid_copies
 
     for load in loads[2:]:

time: 35.2 us -> 35.4 us (level)
  no operation moved by 1% of the time
where the time goes in v7:
time: 35.4 us; the launch traced here: 35.2 us
  Pallas kernels  34.6 us (98%)
  local copies, waits for them, and re-layouts  0.63 us (2%)
    pallas_call x1, Pallas kernels, fused(): pl.pallas_call(functools.partial(fused_kernel, axes), out_shape=pltpu.VME...  34.6 us

profile of v7, /device:TPU:0, one launch (start us, length us, event | category | flops | bytes accessed | tf_op | source)
XLA Modules:
  0.0 35.2 jit_solution(1362171849862749230)
XLA Ops:
  0.0 34.6 %encoder_level.1 = bf16[1,128,256]{2,1,0:T(8,128)(2,1)S(1)} custom-call(bf16[512,256]{1,0:T(8,128)(2,1)} %features_hbm.1, s32[1,512]{1,0:T(1,128)} %scan_order_hbm.1, s32[16,27]{1,0:T(8,128)} %kernel_map_hbm.1, s32[2,2]{1,0:T(2,128)} %halo_send_hbm.1, s32[1,16]{1,0:T(1,128)} %bitcast.11, bf16[3456,256]{1,0:T(8,128)(2,1)} %bitcast.9, ...), custom_call_target="tpu_custom_call" | custom-call | tf_op jit(solution)/shard_map/encoder_level/pallas_call | solution.py:488
  34.6 0.6 %copy.16 = bf16[1,128,256]{2,1,0:T(8,128)(2,1)} copy(bf16[1,128,256]{2,1,0:T(8,128)(2,1)S(1)} %encoder_level.1) | data formatting | bytes 131072
